TPU v7x, 512 devices: a whole 4x4x16 slice. The times are simulated.
512 devices in a mesh: frames: 64 (over z, y), strips: 8 (over x, core).
Axes of the slice: x: 4, y: 4, z: 16, core: 2. Of those that a mesh axis runs over, the one named last changes fastest.
Arguments:
- raw_frames: bfloat16 [4096, 512, 512], P('frames', 'strips'), may hold values from -24 to 24
- dark_frame: float32 [512, 512], P('strips'), may hold values from -6 to 6
- dead_mask: int32 [512, 512], P('strips'), may hold values 0 or 1
- frame_group: int32 [4096], P('frames'), may hold values from 0 to 7
- prior_sigma: float32 [128], replicated, may hold values from 0.2 to 0.5
- start_rotation: float32 [128, 128], replicated, as said below
- basis: bfloat16 [262144, 128], P(('strips', 'frames')), may hold values from -0.01171875 to 0.01171875
Outputs:
- new_basis: bfloat16 [262144, 128], P(('strips', 'frames'))
- new_coeffs: float32 [4096, 128], P('frames')
- new_sigma: float32 [128], replicated
Inputs may be any that keep to these rules, and one draw needn't show every extreme that they name: start_rotation is nonsingular.
All inputs are finite; a program needn't handle non-finite values. No bound on the sum of `dead_mask` on one device may be relied on, other than what follows from the above.
Results may differ from a plain program's by a relative error of at most 0.0071.
Values may be sent and summed in bfloat16 or wider, within the bound.
A program may use at most 64 MiB of HBM per device.

v0:
```python
import jax
import jax.numpy as jnp
from jax import lax
from jax.sharding import PartitionSpec as P

GROUPS = 8
ITERS = 4
BLUR_TAPS = (1.0 / 64, 6.0 / 64, 15.0 / 64, 20.0 / 64, 15.0 / 64, 6.0 / 64, 1.0 / 64)
DECAY_RATE = 0.7


def extended(shard, sides, width):
    for axis, dim in sides:
        size, length = (lax.axis_size(axis), shard.shape[dim])
        up = [(i, (i + 1) % size) for i in range(size - 1)]
        down = [(j, i) for i, j in up]
        last = lax.slice_in_dim(shard, length - width, length, axis=dim)
        first = lax.slice_in_dim(shard, 0, width, axis=dim)
        before = lax.ppermute(last, axis, up)
        after = lax.ppermute(first, axis, down)
        shard = jnp.concatenate([before, shard, after], axis=dim)
    return shard


def orthonormalize(product):
    normal = jnp.dot(product.T, product, precision=lax.Precision.HIGHEST)
    factor = jnp.linalg.cholesky(normal)
    return lax.linalg.triangular_solve(
        factor, product, left_side=False, lower=True, transpose_a=True
    )


def body(raw_frames, dark_frame, dead_mask, frame_group, prior_sigma, start_rotation, basis):
    frame_count, strip_rows, columns = raw_frames.shape
    corrected = (
        (raw_frames.astype(jnp.float32) - dark_frame) * (1 - dead_mask).astype(jnp.float32)
    ).astype(jnp.bfloat16)
    position = jnp.arange(columns)
    offsets = position[None, :] - position[:, None]
    banded = jnp.zeros((columns, columns), jnp.float32)
    for shift_by in range(-3, 4):
        banded = banded + jnp.where(offsets == shift_by, BLUR_TAPS[shift_by + 3], 0.0)
    banded = banded.astype(jnp.bfloat16)
    column_blur = jnp.dot(
        corrected.reshape(frame_count * strip_rows, columns),
        banded,
        preferred_element_type=jnp.float32,
    )
    column_blur = column_blur.reshape(frame_count, strip_rows, columns)
    padded = extended(column_blur, (("strips", 1),), 3)
    row_blur = BLUR_TAPS[0] * padded[:, 0:strip_rows, :]
    for offset in range(1, 7):
        row_blur = row_blur + BLUR_TAPS[offset] * padded[:, offset : offset + strip_rows, :]
    frame_weight = jnp.power(
        jnp.float32(DECAY_RATE), (GROUPS - 1 - frame_group).astype(jnp.float32)
    )
    weighted = (
        (frame_weight[:, None, None] * row_blur)
        .astype(jnp.bfloat16)
        .reshape(frame_count, strip_rows * columns)
    )
    partial_value = jnp.dot(
        weighted,
        lax.all_gather(basis, "frames", axis=0, tiled=True),
        preferred_element_type=jnp.float32,
    )
    coeffs = lax.psum(partial_value, "strips")
    total_frames = frame_count * lax.axis_size("frames")
    local_gram = jnp.dot(coeffs.T, coeffs, precision=lax.Precision.HIGHEST)
    summed_gram = lax.psum(local_gram, "frames")
    gram = jnp.diag(prior_sigma * prior_sigma) + summed_gram / total_frames
    rotation = start_rotation
    for step in range(ITERS):
        rotation = orthonormalize(jnp.dot(gram, rotation, precision=lax.Precision.HIGHEST))
    new_coeffs = jnp.dot(coeffs, rotation, precision=lax.Precision.HIGHEST)
    new_basis = jnp.dot(
        basis.astype(jnp.float32), rotation, precision=lax.Precision.HIGHEST
    ).astype(jnp.bfloat16)
    curved = jnp.dot(gram, rotation, precision=lax.Precision.HIGHEST)
    new_sigma = jnp.sqrt(jnp.sum(rotation * curved, axis=0))
    return (new_basis, new_coeffs, new_sigma)


def solution(mesh):
    placed = (
        P("frames", "strips", None),
        P("strips", None),
        P("strips", None),
        P("frames"),
        P(),
        P(),
        P(("strips", "frames"), None),
    )
    return jax.shard_map(
        body,
        mesh=mesh,
        in_specs=placed,
        out_specs=(P(("strips", "frames"), None), P("frames", None), P()),
        check_vma=False,
    )
```

profile of v0, /device:TPU:2, one launch (start us, length us, event | category | flops | bytes accessed | tf_op | source)
XLA Modules:
  0.0 562.9 jit_solution(2204300600447689643)
XLA Ops:
  7.2 0.7 all-gather.2.cloned.1.call-update
  8.0 0.9 subtract_convert_fusion
  8.9 4.7 fusion.18
  13.6 0.2 fusion.85
  13.9 1.9 collective-permute-start
  15.8 3.6 collective-permute-start.1
  19.5 4.9 collective-permute-done
  24.4 1.8 collective-permute-done.1
  26.1 8.9 %fusion.5 = bf16[64,64,512]{2,1,0:T(8,128)(2,1)S(1)} fusion(f32[64,64,512]{2,1,0:T(8,128)S(1)} %fusion.18, f32[64,3,512]{2,1,0:T(4,128)S(1)} %collective-permute-done.1, f32[64,3,512]{2,1,0:T(4,128)S(1)} %collective-permute-done, f32[64]{0:T(128)S(1)} %convert_power_fusion), kind=kLoop, calls=%fused_computation.13 | loop fusion | flops 44040192 | bytes 13369600 | tf_op jit(solution)/shard_map/convert_element_type | solution.py:59
  35.0 4.5 copy.15
  39.6 132.9 %all-gather.2.cloned.1.call-done = bf16[32768,128]{1,0:T(8,128)(2,1)} async-done(((bf16[512,128]{1,0:T(8,128)(2,1)}), bf16[32768,128]{1,0:T(8,128)(2,1)}) %all-gather.2.cloned.1.call-update) | async-done | bytes 8388624 | tf_op jit(solution)/shard_map/all_gather | solution.py:64
  172.4 6.3 %fusion.86 = f32[64,128]{1,0:T(8,128)S(1)} fusion(bf16[64,32768]{1,0:T(8,128)(2,1)} %bitcast.76, bf16[32768,128]{1,0:T(8,128)(2,1)} %all-gather.2.cloned.1.call-done), kind=kOutput, calls=%fused_computation.116 | convolution fusion | flops 536870912 | bytes 12615680 | tf_op jit(solution)/shard_map/dot_general | solution.py:62
  178.7 20.7 %psum.14 = f32[64,128]{1,0:T(8,128)S(1)} all-reduce(f32[64,128]{1,0:T(8,128)S(1)} %fusion.86), channel_id=1, replica_groups=mesh['frames'=64,'strips'=8] {'strips'}, use_global_device_ids=true, to_apply=%region_0.1 | all-reduce | flops 8192 | bytes 65536 | tf_op jit(solution)/shard_map/psum | solution.py:67
  199.4 0.9 fusion.87
  200.4 253.0 %all-reduce.2.cloned.1.call-done = f32[128,128]{1,0:T(8,128)} async-done(((f32[128,128]{1,0:T(8,128)}), f32[128,128]{1,0:T(8,128)}) %all-reduce.2.cloned.1.call-update) | async-done | bytes 65552 | tf_op jit(solution)/shard_map/psum | solution.py:70
  453.4 1.1 fusion.83
  454.5 0.3 fusion.88
  454.9 11.7 %cholesky.74 = f32[128,128]{1,0:T(8,128)S(1)} custom-call(f32[128,128]{1,0:T(8,128)S(1)} %fusion.55), custom_call_target="Cholesky" | custom-call | tf_op jit(solution)/shard_map/jit(cholesky)/cholesky | solution.py:27
  466.6 0.6 compare_reduce_fusion.3
  467.3 0.7 fusion.44
  468.0 9.8 %custom-call.8 = f32[1,128,128]{1,2,0:T(8,128)S(1)} custom-call(f32[1,128,128]{2,1,0:T(8,128)S(1)} %fusion.44), custom_call_target="InvertDiagBlocksLowerTriangular" | custom-call | tf_op jit(solution)/shard_map/triangular_solve/custom-call.0 | solution.py:28
  477.8 0.3 convolution_bitcast_fusion.3
  478.1 1.1 fusion.81
  479.2 0.3 fusion.89
  479.6 11.7 %cholesky.85 = f32[128,128]{1,0:T(8,128)S(1)} custom-call(f32[128,128]{1,0:T(8,128)S(1)} %fusion.53), custom_call_target="Cholesky" | custom-call | tf_op jit(solution)/shard_map/jit(cholesky)/cholesky | solution.py:27
  491.4 0.6 compare_reduce_fusion.2
  492.0 0.7 fusion.45
  492.7 10.0 %custom-call.9 = f32[1,128,128]{1,2,0:T(8,128)S(1)} custom-call(f32[1,128,128]{2,1,0:T(8,128)S(1)} %fusion.45), custom_call_target="InvertDiagBlocksLowerTriangular" | custom-call | tf_op jit(solution)/shard_map/triangular_solve/custom-call.0 | solution.py:28
  502.7 0.3 convolution_bitcast_fusion.2
  503.0 1.1 fusion.79
  504.1 0.3 fusion.90
  504.5 11.7 %cholesky.96 = f32[128,128]{1,0:T(8,128)S(1)} custom-call(f32[128,128]{1,0:T(8,128)S(1)} %fusion.51), custom_call_target="Cholesky" | custom-call | tf_op jit(solution)/shard_map/jit(cholesky)/cholesky | solution.py:27
  516.3 0.6 compare_reduce_fusion.1
  516.9 0.7 fusion.46
  517.6 9.8 %custom-call.10 = f32[1,128,128]{1,2,0:T(8,128)S(1)} custom-call(f32[1,128,128]{2,1,0:T(8,128)S(1)} %fusion.46), custom_call_target="InvertDiagBlocksLowerTriangular" | custom-call | tf_op jit(solution)/shard_map/triangular_solve/custom-call.0 | solution.py:28
  527.4 0.3 convolution_bitcast_fusion.1
  527.7 1.1 fusion.77
  528.8 0.3 fusion.91
  529.2 11.7 %cholesky.107 = f32[128,128]{1,0:T(8,128)S(1)} custom-call(f32[128,128]{1,0:T(8,128)S(1)} %fusion.49), custom_call_target="Cholesky" | custom-call | tf_op jit(solution)/shard_map/jit(cholesky)/cholesky | solution.py:27
  541.0 0.6 compare_reduce_fusion
  541.6 0.7 fusion.47
  542.3 10.0 %custom-call.11 = f32[1,128,128]{1,2,0:T(8,128)S(1)} custom-call(f32[1,128,128]{2,1,0:T(8,128)S(1)} %fusion.47), custom_call_target="InvertDiagBlocksLowerTriangular" | custom-call | tf_op jit(solution)/shard_map/triangular_solve/custom-call.0 | solution.py:28
  552.3 0.2 convolution_bitcast_fusion
  552.5 0.8 fusion.92
  553.3 0.3 fusion.21
  553.6 1.1 fusion.22
  554.7 0.5 sqrt.3
  555.3 0.8 copy.14
  (25 shorter events, 0.7 us)
Async XLA Ops:
  7.2 446.2 %copy-start = (f32[128,128]{1,0:T(8,128)S(1)}, f32[128,128]{1,0:T(8,128)}, u32[]{:S(2)}) copy-start(f32[128,128]{1,0:T(8,128)} %param.15) | copy-start | bytes 196612
  7.2 165.3 %all-gather.2.cloned.1.call-start = ((), (), s32[]{:S(2)}) async-start(), calls=%async_computation | async-start | bytes 8519680 | tf_op jit(solution)/shard_map/all_gather | solution.py:64
  7.9 445.5 %all-reduce.2.cloned.1.call-start = ((), (), s32[]{:S(2)}) async-start(), calls=%async_computation.1 | async-start | bytes 131072 | tf_op jit(solution)/shard_map/psum | solution.py:70
  8.9 10.6 %copy-start.2 = (s32[64]{0:T(128)S(1)}, s32[64]{0:T(128)}, u32[]{:S(2)}) copy-start(s32[64]{0:T(128)} %param.13) | copy-start | bytes 772
  13.9 10.5 %collective-permute-start = (f32[64,3,512]{2,1,0:T(4,128)S(1)}, f32[64,3,512]{2,1,0:T(4,128)S(1)}, u32[]{:S(2)}, u32[]{:S(2)}) collective-permute-start(f32[64,3,512]{2,1,0:T(4,128)S(1)} %get-tuple-element.8), channel_id=1, source_target_pairs={{0,1},{1,2},{2,3},{3,4},{4,5},{5,6},{6,7},{8,9},{9,10},{10,11},{11... | collective-permute-start | bytes 1179656 | tf_op jit(solution)/shard_map/ppermute | solution.py:19
  15.8 10.3 %collective-permute-start.1 = (f32[64,3,512]{2,1,0:T(4,128)S(1)}, f32[64,3,512]{2,1,0:T(4,128)S(1)}, u32[]{:S(2)}, u32[]{:S(2)}) collective-permute-start(f32[64,3,512]{2,1,0:T(4,128)S(1)} %get-tuple-element.9), channel_id=1, source_target_pairs={{1,0},{2,1},{3,2},{4,3},{5,4},{6,5},{7,6},{9,8},{10,9},{11,10},{12... | collective-permute-start | bytes 1179656 | tf_op jit(solution)/shard_map/ppermute | solution.py:20
  172.4 27.9 %copy-start.3 = (f32[128]{0:T(128)S(1)}, f32[128]{0:T(128)}, u32[]{:S(2)}) copy-start(f32[128]{0:T(128)} %param.14) | copy-start | bytes 1540
  172.4 380.9 %copy-start.1 = (bf16[512,128]{1,0:T(8,128)(2,1)S(1)}, bf16[512,128]{1,0:T(8,128)(2,1)}, u32[]{:S(2)}) copy-start(bf16[512,128]{1,0:T(8,128)(2,1)} %param.16) | copy-start | bytes 393220
Sparse Core Ops, SparseCore 0:
  11.0 161.4 all-gather.1
  200.5 252.8 all-reduce.1
where the time goes:
time: 563 us
  waiting for transfers between devices  393 us (70%)
  other arithmetic  102 us (18%)
  matrix products  20.9 us (4%)
  blocking collectives  20.7 us (4%)
  between operations  14.3 us (3%)
  local copies, waits for them, and re-layouts  6.45 us (1%)
  starting transfers between devices  5.64 us (1%)
    psum x1, waiting for transfers between devices, body(): summed_gram = lax.psum(local_gram, 'frames')  253 us
    all_gather x1, waiting for transfers between devices, body(): lax.all_gather(basis, 'frames', axis=0, tiled=True)  133 us
    another operation x12, other arithmetic, orthonormalize(): factor = jnp.linalg.cholesky(normal)  49.6 us
    another operation x8, other arithmetic, orthonormalize(): lax.linalg.triangular_solve(factor, product, left_side=False, lower=True,...  42.2 us
    psum x1, blocking collectives, body(): coeffs = lax.psum(partial_value, 'strips')  20.7 us
  transfers between devices with their start and end apart: 4, of which 4 were waited for; matrix products, arithmetic and copies ran while one was open for 3% of the time, Pallas kernels for 0%

commit v1 on v0

--- a/solution.py
+++ b/solution.py
@@ -7,6 +7,11 @@
 ITERS = 4
 BLUR_TAPS = (1.0 / 64, 6.0 / 64, 15.0 / 64, 20.0 / 64, 15.0 / 64, 6.0 / 64, 1.0 / 64)
 DECAY_RATE = 0.7
+
+
+def tiled_gather(x, axis, dim):
+    copies = jnp.concatenate([x] * lax.axis_size(axis), axis=dim)
+    return lax.all_to_all(copies, axis, dim, dim, tiled=True)
 
 
 def extended(shard, sides, width):
@@ -60,9 +65,7 @@
         .reshape(frame_count, strip_rows * columns)
     )
     partial_value = jnp.dot(
-        weighted,
-        lax.all_gather(basis, "frames", axis=0, tiled=True),
-        preferred_element_type=jnp.float32,
+        weighted, tiled_gather(basis, "frames", 0), preferred_element_type=jnp.float32
     )
     coeffs = lax.psum(partial_value, "strips")
     total_frames = frame_count * lax.axis_size("frames")

time: 563 us -> 828 us (1.47)
  waiting for transfers between devices: 393 us -> 600 us
  local copies, waits for them, and re-layouts: 6.45 us -> 35.4 us
  starting transfers between devices: 5.64 us -> 25.3 us
    all_to_all x0 -> x1, waiting for transfers between devices: none -> 343 us  [tiled_gather(): return lax.all_to_all(copies, axis, dim, dim, tiled=True)]
    all_gather x1 -> x0, waiting for transfers between devices: 133 us -> none  [body(): lax.all_gather(basis, 'frames', axis=0, tiled=True)]
    unnamed x10 -> x78, local copies, waits for them, and re-layouts: 5.33 us -> 34.2 us
    all_to_all x0 -> x1, starting transfers between devices: none -> 19.1 us  [tiled_gather(): return lax.all_to_all(copies, axis, dim, dim, tiled=True)]
  transfers between devices with their start and end apart: 4 -> 4, of which waited for: 4 -> 4; matrix products, arithmetic and copies ran while one was open for 3% -> 2% of each run, Pallas kernels for 0% -> 0%
where the time goes in v1:
time: 828 us; the launch traced here: 823 us
  waiting for transfers between devices  600 us (72%)
  other arithmetic  102 us (12%)
  local copies, waits for them, and re-layouts  35.4 us (4%)
  starting transfers between devices  25.3 us (3%)
  matrix products  24.2 us (3%)
  blocking collectives  20.8 us (3%)
  between operations  15 us (2%)
    all_to_all x1, waiting for transfers between devices, tiled_gather(): return lax.all_to_all(copies, axis, dim, dim, tiled=True)  343 us
    psum x1, waiting for transfers between devices, body(): summed_gram = lax.psum(local_gram, 'frames')  251 us
    another operation x12, other arithmetic, orthonormalize(): factor = jnp.linalg.cholesky(normal)  49.6 us
    another operation x8, other arithmetic, orthonormalize(): lax.linalg.triangular_solve(factor, product, left_side=False, lower=True,...  42.3 us
    unnamed x78, local copies, waits for them, and re-layouts  34.2 us
    psum x1, blocking collectives, body(): coeffs = lax.psum(partial_value, 'strips')  20.8 us
    all_to_all x1, starting transfers between devices, tiled_gather(): return lax.all_to_all(copies, axis, dim, dim, tiled=True)  19.1 us
  transfers between devices with their start and end apart: 4, of which 4 were waited for; matrix products, arithmetic and copies ran while one was open for 2% of the time, Pallas kernels for 0%

profile of v1, /device:TPU:2, one launch (start us, length us, event | category | flops | bytes accessed | tf_op | source)
XLA Modules:
  0.0 822.6 jit_solution(11574078588855065247)
XLA Ops:
  7.2 1.0 constant_dynamic-update-slice_fusion.63
  8.2 0.9 constant_dynamic-update-slice_fusion.62
  9.1 0.9 constant_dynamic-update-slice_fusion.61
  10.0 0.9 constant_dynamic-update-slice_fusion.60
  11.0 0.9 constant_dynamic-update-slice_fusion.59
  11.9 0.9 constant_dynamic-update-slice_fusion.58
  12.8 0.9 constant_dynamic-update-slice_fusion.57
  13.7 0.9 constant_dynamic-update-slice_fusion.56
  14.7 0.9 constant_dynamic-update-slice_fusion.55
  15.6 0.9 constant_dynamic-update-slice_fusion.54
  16.5 0.9 constant_dynamic-update-slice_fusion.53
  17.4 0.9 constant_dynamic-update-slice_fusion.52
  18.4 0.9 constant_dynamic-update-slice_fusion.51
  20.2 0.9 constant_dynamic-update-slice_fusion.49
  22.1 0.9 constant_dynamic-update-slice_fusion.47
  23.9 0.9 constant_dynamic-update-slice_fusion.45
  24.9 0.9 constant_dynamic-update-slice_fusion.44
  26.7 0.9 constant_dynamic-update-slice_fusion.42
  28.6 0.9 constant_dynamic-update-slice_fusion.40
  30.4 0.9 constant_dynamic-update-slice_fusion.38
  31.4 0.9 constant_dynamic-update-slice_fusion.37
  33.2 0.9 constant_dynamic-update-slice_fusion.35
  35.1 0.9 constant_dynamic-update-slice_fusion.33
  37.8 3.2 copy-done.2
  41.0 19.1 %all-to-all-start = ((bf16[64,512,128]{2,1,0:T(8,128)(2,1)}), bf16[64,512,128]{2,1,0:T(8,128)(2,1)}, u32[]{:S(2)}, u32[]{:S(2)}) async-start(bf16[64,512,128]{2,1,0:T(8,128)(2,1)} %bitcast.76), calls=%async_computation | async-start | bytes 16777216 | tf_op jit(solution)/shard_map/all_to_all | solution.py:14
  60.3 4.7 fusion.18
  65.2 1.9 collective-permute-start
  67.2 4.2 collective-permute-start.1
  71.4 4.4 collective-permute-done
  75.7 1.8 collective-permute-done.1
  77.5 9.7 %fusion.5 = bf16[64,64,512]{2,1,0:T(8,128)(2,1)} fusion(f32[64,64,512]{2,1,0:T(8,128)S(1)} %fusion.18, f32[64,3,512]{2,1,0:T(4,128)S(1)} %collective-permute-done.1, f32[64,3,512]{2,1,0:T(4,128)S(1)} %collective-permute-done, f32[64]{0:T(128)S(1)} %convert_power_fusion), kind=kLoop, calls=%fused_computation.13 | loop fusion | flops 44040192 | bytes 13369600 | tf_op jit(solution)/shard_map/convert_element_type | solution.py:64
  87.2 342.7 %all-to-all-done = bf16[64,512,128]{2,1,0:T(8,128)(2,1)} async-done(((bf16[64,512,128]{2,1,0:T(8,128)(2,1)}), bf16[64,512,128]{2,1,0:T(8,128)(2,1)}, u32[]{:S(2)}, u32[]{:S(2)}) %all-to-all-start) | async-done | bytes 8388640 | tf_op jit(solution)/shard_map/all_to_all | solution.py:14
  429.9 9.6 %fusion.25 = f32[64,128]{1,0:T(8,128)S(1)} fusion(bf16[64,512,128]{2,1,0:T(8,128)(2,1)} %all-to-all-done, bf16[64,64,512]{2,1,0:T(8,128)(2,1)} %fusion.5), kind=kOutput, calls=%fused_computation.42 | convolution fusion | flops 536870912 | bytes 12615680 | tf_op jit(solution)/shard_map/dot_general | solution.py:67
  439.6 20.8 %psum.14 = f32[64,128]{1,0:T(8,128)S(1)} all-reduce(f32[64,128]{1,0:T(8,128)S(1)} %fusion.25), channel_id=1, replica_groups=mesh['frames'=64,'strips'=8] {'strips'}, use_global_device_ids=true, to_apply=%region_0.1 | all-reduce | flops 8192 | bytes 65536 | tf_op jit(solution)/shard_map/psum | solution.py:70
  461.3 251.5 %all-reduce.2.cloned.1.call-done = f32[128,128]{1,0:T(8,128)} async-done(((f32[128,128]{1,0:T(8,128)}), f32[128,128]{1,0:T(8,128)}) %all-reduce.2.cloned.1.call-update) | async-done | bytes 65552 | tf_op jit(solution)/shard_map/psum | solution.py:73
  712.8 1.1 fusion.88
  714.3 11.7 %cholesky.74 = f32[128,128]{1,0:T(8,128)S(1)} custom-call(f32[128,128]{1,0:T(8,128)S(1)} %fusion.60), custom_call_target="Cholesky" | custom-call | tf_op jit(solution)/shard_map/jit(cholesky)/cholesky | solution.py:32
  727.4 9.8 %custom-call.8 = f32[1,128,128]{1,2,0:T(8,128)S(1)} custom-call(f32[1,128,128]{2,1,0:T(8,128)S(1)} %fusion.49), custom_call_target="InvertDiagBlocksLowerTriangular" | custom-call | tf_op jit(solution)/shard_map/triangular_solve/custom-call.0 | solution.py:33
  737.5 1.1 fusion.86
  739.0 11.7 %cholesky.85 = f32[128,128]{1,0:T(8,128)S(1)} custom-call(f32[128,128]{1,0:T(8,128)S(1)} %fusion.58), custom_call_target="Cholesky" | custom-call | tf_op jit(solution)/shard_map/jit(cholesky)/cholesky | solution.py:32
  752.1 10.0 %custom-call.9 = f32[1,128,128]{1,2,0:T(8,128)S(1)} custom-call(f32[1,128,128]{2,1,0:T(8,128)S(1)} %fusion.50), custom_call_target="InvertDiagBlocksLowerTriangular" | custom-call | tf_op jit(solution)/shard_map/triangular_solve/custom-call.0 | solution.py:33
  762.4 1.1 fusion.84
  763.9 11.7 %cholesky.96 = f32[128,128]{1,0:T(8,128)S(1)} custom-call(f32[128,128]{1,0:T(8,128)S(1)} %fusion.56), custom_call_target="Cholesky" | custom-call | tf_op jit(solution)/shard_map/jit(cholesky)/cholesky | solution.py:32
  777.0 9.8 %custom-call.10 = f32[1,128,128]{1,2,0:T(8,128)S(1)} custom-call(f32[1,128,128]{2,1,0:T(8,128)S(1)} %fusion.51), custom_call_target="InvertDiagBlocksLowerTriangular" | custom-call | tf_op jit(solution)/shard_map/triangular_solve/custom-call.0 | solution.py:33
  787.1 1.1 fusion.82
  788.6 11.7 %cholesky.107 = f32[128,128]{1,0:T(8,128)S(1)} custom-call(f32[128,128]{1,0:T(8,128)S(1)} %fusion.54), custom_call_target="Cholesky" | custom-call | tf_op jit(solution)/shard_map/jit(cholesky)/cholesky | solution.py:32
  801.7 10.0 %custom-call.11 = f32[1,128,128]{1,2,0:T(8,128)S(1)} custom-call(f32[1,128,128]{2,1,0:T(8,128)S(1)} %fusion.52), custom_call_target="InvertDiagBlocksLowerTriangular" | custom-call | tf_op jit(solution)/shard_map/triangular_solve/custom-call.0 | solution.py:33
  813.1 1.1 fusion.24
  (93 shorter events, 20.6 us)
Async XLA Ops:
  7.2 705.6 %copy-start = (f32[128,128]{1,0:T(8,128)S(1)}, f32[128,128]{1,0:T(8,128)}, u32[]{:S(2)}) copy-start(f32[128,128]{1,0:T(8,128)} %param.15) | copy-start | bytes 196612
  7.2 29.7 %copy-start.1 = (bf16[512,128]{1,0:T(8,128)(2,1)S(1)}, bf16[512,128]{1,0:T(8,128)(2,1)}, u32[]{:S(2)}) copy-start(bf16[512,128]{1,0:T(8,128)(2,1)} %param.16) | copy-start | bytes 393220
  37.8 3.2 copy-start.2
  41.0 19.2 %copy-start.3 = (s32[64,512]{1,0:T(8,128)S(1)}, s32[64,512]{1,0:T(8,128)}, u32[]{:S(2)}) copy-start(s32[64,512]{1,0:T(8,128)} %param.12) | copy-start | bytes 393220
  41.0 19.2 %copy-start.4 = (f32[64,512]{1,0:T(8,128)S(1)}, f32[64,512]{1,0:T(8,128)}, u32[]{:S(2)}) copy-start(f32[64,512]{1,0:T(8,128)} %param.11) | copy-start | bytes 393220
  41.0 388.9 %all-to-all-start = ((bf16[64,512,128]{2,1,0:T(8,128)(2,1)}), bf16[64,512,128]{2,1,0:T(8,128)(2,1)}, u32[]{:S(2)}, u32[]{:S(2)}) async-start(bf16[64,512,128]{2,1,0:T(8,128)(2,1)} %bitcast.76), calls=%async_computation | async-start | bytes 16777216 | tf_op jit(solution)/shard_map/all_to_all | solution.py:14
  60.2 652.7 %all-reduce.2.cloned.1.call-start = ((), (), s32[]{:S(2)}) async-start(), calls=%async_computation.1 | async-start | bytes 131072 | tf_op jit(solution)/shard_map/psum | solution.py:73
  60.2 11.1 %copy-start.5 = (s32[64]{0:T(128)S(1)}, s32[64]{0:T(128)}, u32[]{:S(2)}) copy-start(s32[64]{0:T(128)} %param.13) | copy-start | bytes 772
  65.2 10.5 %collective-permute-start = (f32[64,3,512]{2,1,0:T(4,128)S(1)}, f32[64,3,512]{2,1,0:T(4,128)S(1)}, u32[]{:S(2)}, u32[]{:S(2)}) collective-permute-start(f32[64,3,512]{2,1,0:T(4,128)S(1)} %get-tuple-element.8), channel_id=1, source_target_pairs={{0,1},{1,2},{2,3},{3,4},{4,5},{5,6},{6,7},{8,9},{9,10},{10,11},{11... | collective-permute-start | bytes 1179656 | tf_op jit(solution)/shard_map/ppermute | solution.py:24
  67.2 10.3 %collective-permute-start.1 = (f32[64,3,512]{2,1,0:T(4,128)S(1)}, f32[64,3,512]{2,1,0:T(4,128)S(1)}, u32[]{:S(2)}, u32[]{:S(2)}) collective-permute-start(f32[64,3,512]{2,1,0:T(4,128)S(1)} %get-tuple-element.9), channel_id=1, source_target_pairs={{1,0},{2,1},{3,2},{4,3},{5,4},{6,5},{7,6},{9,8},{10,9},{11,10},{12... | collective-permute-start | bytes 1179656 | tf_op jit(solution)/shard_map/ppermute | solution.py:25
  87.2 374.1 %copy-start.6 = (f32[128]{0:T(128)S(1)}, f32[128]{0:T(128)}, u32[]{:S(2)}) copy-start(f32[128]{0:T(128)} %param.14) | copy-start | bytes 1540
Sparse Core Ops, SparseCore 0:
  461.4 251.3 all-reduce.1
